TPU v7x, 256 devices: a whole 4x4x8 slice. The times are simulated.
256 devices in a mesh: bubble: 16 (over y_hi, z), panel: 16 (over y_lo, x, core).
Axes of the slice: x: 4, y: 4 (y_hi: 2, y_lo: 2; y = y_hi * 2 + y_lo), z: 8, core: 2. Of those that a mesh axis runs over, the one named last changes fastest.
Arguments:
- density: float32 [128, 12288], P('bubble', 'panel'), may hold values from -6 to 6
- right_side: float32 [128, 12288], P('bubble', 'panel'), may hold values from -6 to 6
- inv_diag: bfloat16 [128, 96, 128, 128], P('bubble', 'panel')
- near_vals: bfloat16 [128, 96, 4, 128, 128], P('bubble', 'panel'), may hold values from -0.25 to 0.25
- near_bubble: int32 [128, 96, 4], P('bubble', 'panel'), may hold values from 0 to 127, as said below
- near_block: int32 [128, 96, 4], P('bubble', 'panel'), may hold values from 0 to 95
- near_count: int32 [128, 96], P('bubble', 'panel'), may hold values from 1 to 4, as said below
- colour: int32 [128], P('bubble'), may hold values from 0 to 1
- moment_map: bfloat16 [128, 16, 12288], P('bubble', None, 'panel'), may hold values from -0.0546875 to 0.0546875
- spread_map: bfloat16 [128, 16, 12288], P('bubble', None, 'panel'), may hold values from -0.125 to 0.125
- centres: float32 [3, 128], replicated, may hold values from 0.2 to 6
Outputs:
- relaxed: float32 [128, 12288], P('bubble', 'panel')
Inputs may be any that keep to these rules, and one draw needn't show every extreme that they name: `near_bubble`: every slot of bubble b names a bubble within 8 of b. `near_count`: the first row block of every bubble uses all 4 slots.
All inputs are finite; a program needn't handle non-finite values.
Results may differ from a plain program's by a relative error of at most 0.0041.
Values may be sent and summed in bfloat16 or wider, within the bound.
No kernel may reach another device: no remote copies, remote signals or barrier semaphores. Data moves between devices by JAX's collectives and lax.ppermute only.
A program may use at most 64 MiB of HBM per device.

v0:
```python
import functools

import jax
import jax.numpy as jnp
from jax import lax
from jax.experimental import pallas as pl
from jax.experimental.pallas import tpu as pltpu
from jax.sharding import PartitionSpec as P


NT = (((1,), (1,)), ((), ()))
NN = (((1,), (0,)), ((), ()))


def row_ids(shape):
    return lax.broadcasted_iota(jnp.int32, shape, 0)


def emit_message(tiles, moment_map, message):
    bub, lanes = tiles[0].shape
    peers, slots = message.shape[:2]
    k = lanes // bub
    dens = jnp.concatenate(tiles, axis=1).astype(jnp.bfloat16)
    cross = lax.dot_general(dens, moment_map[...], NT, preferred_element_type=jnp.float32)
    rows = row_ids((bub, lanes))
    own = lax.broadcasted_iota(jnp.int32, (bub, lanes), 1) // k == rows
    share = jnp.sum(jnp.where(own, cross, 0.0), axis=0, keepdims=True)
    top = share.astype(jnp.bfloat16).astype(jnp.float32)
    rest = share - top
    mid = rest.astype(jnp.bfloat16).astype(jnp.float32)
    low = rest - mid
    parts = jnp.where(
        rows == 0, top, jnp.where(rows == 1, mid, jnp.where(rows == 2, low, 0.0))
    ).astype(jnp.bfloat16)
    blocks = [t.astype(jnp.bfloat16) for t in tiles] + [parts]
    for p in range(peers):
        for j in range(slots):
            message[p, j] = blocks[j]


def first_kernel(density_hbm, map_hbm, message, density, moment_map, sems):
    copies = [
        pltpu.make_async_copy(map_hbm, moment_map, sems.at[0]),
        pltpu.make_async_copy(density_hbm, density, sems.at[1]),
    ]
    for c in copies:
        c.start()
    for c in copies:
        c.wait()
    n = message.shape[1] - 1
    w = message.shape[3]
    tiles = [density[:, j * w : (j + 1) * w] for j in range(n)]
    emit_message(tiles, moment_map, message)


def moment_kernel(received, out):
    peers, slots = received.shape[:2]
    total = received[0, slots - 1].astype(jnp.float32)
    for p in range(1, peers):
        total = total + received[p, slots - 1].astype(jnp.float32)
    row = jnp.sum(total, axis=0, keepdims=True)
    for g in range(out.shape[0]):
        out[g] = row


def shift_of(power):
    assert power & (power - 1) == 0
    return power.bit_length() - 1


def far_weights(centres, first, reach):
    shape = (reach, centres.shape[1])
    rows = row_ids(shape)
    q = lax.broadcasted_iota(jnp.int32, shape, 1)
    theirs = [jnp.broadcast_to(centres[c : c + 1, :], shape) for c in range(3)]
    mine = [jnp.take_along_axis(t, first + rows, axis=1) for t in theirs]
    d0, d1, d2 = (m - t for m, t in zip(mine, theirs))
    mirrored = mine[2] + theirs[2]
    direct_sq = d0 * d0 + d1 * d1 + d2 * d2
    image_sq = d0 * d0 + d1 * d1 + mirrored * mirrored
    kernel = 1.0 / jnp.sqrt(direct_sq + 1.0) + 1.0 / jnp.sqrt(image_sq + 1.0)
    return jnp.where(jnp.abs(first + rows - q) > reach, kernel, 0.0)


def near_kernel(
    colour_now,
    near_bubble,
    near_block,
    near_count,
    colour,
    centres,
    odd_swap,
    own,
    even_swap,
    right_side,
    near_vals,
    rest,
    live,
    *refs,
):
    *weights, sources, vals, sems = refs
    bub, nblk, slots, blk, _ = near_vals.shape
    peers = own.shape[0]
    my_index = lax.axis_index("bubble")
    first = my_index * bub
    even = (my_index & 1) == 0
    none = 3 * peers * nblk * bub

    def copy(b):
        return pltpu.make_async_copy(near_vals.at[b], vals.at[b], sems.at[b])

    for b in range(bub):

        @pl.when(colour[b] == colour_now)
        def _():
            copy(b).start()

    rows = row_ids((bub, blk))
    for o, ref in enumerate((odd_swap, own, even_swap)):
        for p in range(peers):
            for j in range(nblk):
                at = ((o * peers + p) * nblk + j) * bub
                sources[at : at + bub, :] = ref[p, j].astype(jnp.float32)
    sources[none:, :] = jnp.zeros((bub, blk), jnp.float32)
    colours = jnp.zeros((bub, blk), jnp.int32)
    for b in range(bub):
        colours = jnp.where(rows == b, colour[b], colours)
    live[...] = (colours == colour_now).astype(jnp.float32)
    for r in range(nblk):
        rest[r] = right_side[:, r * blk : (r + 1) * blk]
    for table in weights:
        weight = far_weights(centres, first, bub)
        lane = lax.broadcasted_iota(jnp.int32, (bub, blk), 1)
        for q in range(table.shape[0]):
            table[q] = jnp.take_along_axis(weight, q * bub + lane // (blk // bub), axis=1)

    def near_of(b, carry):
        @pl.when(colour[b] == colour_now)
        def _():
            copy(b).wait()
            here = rows == b
            for r in range(nblk):
                picked = []
                for s in range(slots):
                    local = near_bubble[r, s, b] - (first - bub)
                    o = local >> shift_of(bub)
                    o = jnp.where(even, o, 2 - o)
                    row = (o * peers * nblk + near_block[r, s, b]) * bub + (local & (bub - 1))
                    i = jnp.where(s < near_count[b, r], row, none)
                    picked.append(jnp.where(here, sources[pl.ds(i, 1), :], 0.0))
                src = jnp.concatenate(picked, axis=1).astype(jnp.bfloat16)
                block = jnp.concatenate([vals[b, r, s] for s in range(slots)], axis=1)
                rest[r] -= lax.dot_general(src, block, NT, preferred_element_type=jnp.float32)

        return carry

    lax.fori_loop(0, bub, near_of, 0)


def finish_kernel(
    last,
    moments,
    weights,
    rest,
    live,
    spread_map,
    relaxed,
    moment_map,
    inv_diag,
    *refs,
):
    bub, nblk, blk, _ = inv_diag.shape
    k = blk // bub
    out = refs[0]
    rows = row_ids((bub, blk))
    lane = lax.broadcasted_iota(jnp.int32, (bub, blk), 1)

    terms = [weights[q] * moments[q] for q in range(moments.shape[0])]
    while len(terms) > 1:
        terms = [u + v for u, v in zip(terms[::2], terms[1::2])]
    g = terms[0]
    shift = blk // 2
    while shift >= k:
        g = g + pltpu.roll(g, shift, 1)
        shift //= 2
    coeff = jnp.where(lane // k == rows, g, 0.0).astype(jnp.bfloat16)
    far = lax.dot_general(coeff, spread_map[...], NN, preferred_element_type=jnp.float32)

    is_live = live[...] > 0.5
    tiles = []
    for r in range(nblk):
        cols = slice(r * blk, (r + 1) * blk)
        remainder = rest[r] - far[:, cols]
        updated = jnp.zeros((bub, blk), jnp.float32)
        for b in range(0, bub, 2):
            pair = jnp.concatenate(
                [jnp.where(rows == b + h, remainder, 0.0) for h in range(2)], axis=1
            ).astype(jnp.bfloat16)
            block = jnp.concatenate([inv_diag[b, r], inv_diag[b + 1, r]], axis=1)
            updated = updated + lax.dot_general(
                pair, block, NT, preferred_element_type=jnp.float32
            )
        tile = jnp.where(is_live, updated, relaxed[:, cols])
        out[:, cols] = tile
        tiles.append(tile)
    if not last:
        emit_message(tiles, moment_map, refs[1])


VMEM = pl.BlockSpec(memory_space=pltpu.VMEM)
SMEM = pl.BlockSpec(memory_space=pltpu.SMEM)
HBM = pl.BlockSpec(memory_space=pltpu.HBM)


def in_hbm(x):
    return pltpu.with_memory_space_constraint(x, pltpu.HBM)


def limit(mib):
    return pltpu.CompilerParams(vmem_limit_bytes=mib << 20)


def per_device(
    density,
    right_side,
    inv_diag,
    near_vals,
    near_bubble,
    near_block,
    near_count,
    colour,
    moment_map,
    spread_map,
    centres,
):
    bub, nblk, slots, blk, _ = near_vals.shape
    k = moment_map.shape[1]
    panels = nblk * blk
    peers, groups = lax.axis_size("panel"), lax.axis_size("bubble")
    moment_map = moment_map.reshape(bub * k, panels)
    spread_map = spread_map.reshape(bub * k, panels)

    message_shape = jax.ShapeDtypeStruct((peers, nblk + 1, bub, blk), jnp.bfloat16)
    near_shapes = [
        jax.ShapeDtypeStruct((nblk, bub, blk), jnp.float32),
        jax.ShapeDtypeStruct((bub, blk), jnp.float32),
        jax.ShapeDtypeStruct((groups, bub, blk), jnp.float32),
    ]
    relaxed_shape = jax.ShapeDtypeStruct((bub, panels), jnp.float32)
    pairs = [(i, i + 1) for i in range(groups - 1)]
    odd_pairs = [(i, j) for p in pairs[1::2] for i, j in (p, p[::-1])]
    odd_pairs += [(0, groups - 1), (groups - 1, 0)]
    even_pairs = [(i, j) for p in pairs[0::2] for i, j in (p, p[::-1])]

    message = pl.pallas_call(
        first_kernel,
        out_shape=message_shape,
        in_specs=[HBM, HBM],
        out_specs=VMEM,
        scratch_shapes=[
            pltpu.VMEM((bub, panels), jnp.float32),
            pltpu.VMEM((bub * k, panels), jnp.bfloat16),
            pltpu.SemaphoreType.DMA((2,)),
        ],
        compiler_params=limit(2),
        cost_estimate=pl.CostEstimate(flops=1 << 34, bytes_accessed=1 << 20, transcendentals=0),
        name="first",
    )(in_hbm(density), in_hbm(moment_map))
    near_vals = in_hbm(near_vals)
    near_bubble = near_bubble.transpose(1, 2, 0)
    near_block = near_block.transpose(1, 2, 0)
    relaxed = density
    for colour_now in range(2):
        last = colour_now == 1
        received = lax.all_to_all(message, "panel", 0, 0, tiled=True)
        even_swap = lax.ppermute(received, "bubble", even_pairs)
        odd_swap = lax.ppermute(received, "bubble", odd_pairs)
        own_moments = pl.pallas_call(
            moment_kernel,
            out_shape=jax.ShapeDtypeStruct((groups, 1, blk), jnp.float32),
            in_specs=[VMEM],
            out_specs=VMEM,
            compiler_params=limit(2),
            name="moments",
        )(received)
        moments = lax.all_to_all(own_moments, "bubble", 0, 0, tiled=True)
        rest, live, *table = pl.pallas_call(
            functools.partial(near_kernel, colour_now),
            out_shape=near_shapes[: 2 if last else 3],
            in_specs=[SMEM] * 4 + [VMEM] * 5 + [HBM],
            out_specs=[VMEM] * (2 if last else 3),
            scratch_shapes=[
                pltpu.VMEM(((3 * peers * nblk + 1) * bub, blk), jnp.float32),
                pltpu.VMEM((bub, nblk, slots, blk, blk), jnp.bfloat16),
                pltpu.SemaphoreType.DMA((bub,)),
            ],
            compiler_params=limit(12),
        )(
            near_bubble,
            near_block,
            near_count,
            colour,
            centres,
            odd_swap,
            received,
            even_swap,
            right_side,
            near_vals,
        )
        weights = table[0] if table else weights
        outs = pl.pallas_call(
            functools.partial(finish_kernel, last),
            out_shape=[relaxed_shape] if last else [relaxed_shape, message_shape],
            in_specs=[VMEM] * 8,
            out_specs=[VMEM] if last else [VMEM, VMEM],
            compiler_params=limit(4),
        )(moments, weights, rest, live, spread_map, relaxed, moment_map, inv_diag)
        if last:
            (relaxed,) = outs
        else:
            relaxed, message = outs
    return relaxed


def solution(mesh):
    in_specs = (
        P("bubble", "panel"),
        P("bubble", "panel"),
        P("bubble", "panel", None, None),
        P("bubble", "panel", None, None, None),
        P("bubble", "panel", None),
        P("bubble", "panel", None),
        P("bubble", "panel"),
        P("bubble"),
        P("bubble", None, "panel"),
        P("bubble", None, "panel"),
        P(),
    )
    out_specs = P("bubble", "panel")

    return jax.shard_map(
        per_device, mesh=mesh, in_specs=in_specs, out_specs=out_specs, check_vma=False
    )
```

profile of v0, /device:TPU:8, one launch (start us, length us, event | category | flops | bytes accessed | tf_op | source)
XLA Modules:
  0.0 68.2 jit_solution(1409362631787404986)
XLA Ops:
  0.0 1.2 %first.1 = bf16[16,7,8,128]{3,2,1,0:T(8,128)(2,1)S(1)} custom-call(f32[8,768]{1,0:T(8,128)} %relaxed.1, bf16[128,768]{1,0:T(8,128)(2,1)} %bitcast.4), custom_call_target="tpu_custom_call" | custom-call | flops 17179869184 | bytes 1048576 | tf_op jit(solution)/shard_map/first/pallas_call | solution.py:255
  1.2 0.0 copy-start
  1.3 0.0 copy-start.1
  1.3 0.0 copy-start.2
  1.3 0.0 copy-start.6
  1.3 11.8 %all_to_all.20.received.own = bf16[16,7,8,128]{3,2,1,0:T(8,128)(2,1)S(1)} all-to-all(bf16[16,7,8,128]{3,2,1,0:T(8,128)(2,1)S(1)} %first.1), channel_id=1, replica_groups=mesh['bubble'=16,'panel'=16] {'panel'}, dimensions={0} | all-to-all | bytes 458752 | tf_op jit(solution)/shard_map/all_to_all | solution.py:275
  13.1 7.6 %collective-permute-start = (bf16[16,7,8,128]{3,2,1,0:T(8,128)(2,1)S(1)}, bf16[16,7,8,128]{3,2,1,0:T(8,128)(2,1)S(1)}, u32[]{:S(2)}, u32[]{:S(2)}) collective-permute-start(bf16[16,7,8,128]{3,2,1,0:T(8,128)(2,1)S(1)} %all_to_all.20.received.own), channel_id=1, source_target_pairs={{16,32},{32,16},{48,64},{64,48},{80,96},{96,80},{112,128},{128,112... | collective-permute-start | bytes 688136 | tf_op jit(solution)/shard_map/ppermute | solution.py:277
  20.7 0.0 collective-permute-start.1
  20.7 0.6 moments.2
  21.4 4.7 %all-to-all-start.1 = ((f32[16,1,128]{2,1,0:T(1,128)}), f32[16,1,128]{2,1,0:T(1,128)S(1)}, u32[]{:S(2)}, u32[]{:S(2)}) async-start(f32[16,1,128]{2,1,0:T(1,128)} %moments.2), calls=%async_computation.1 | async-start | bytes 16384 | tf_op jit(solution)/shard_map/all_to_all | solution.py:286
  26.1 0.5 collective-permute-done.odd_swap
  26.6 1.5 %collective-permute-done.1.even_swap = bf16[16,7,8,128]{3,2,1,0:T(8,128)(2,1)S(1)} collective-permute-done((bf16[16,7,8,128]{3,2,1,0:T(8,128)(2,1)S(1)}, bf16[16,7,8,128]{3,2,1,0:T(8,128)(2,1)S(1)}, u32[]{:S(2)}, u32[]{:S(2)}) %collective-permute-start.1) | collective-permute-done | bytes 229408 | tf_op jit(solution)/shard_map/ppermute | solution.py:276
  28.2 3.5 %shard_map.109 = (f32[6,8,128]{2,1,0:T(8,128)S(1)}, f32[8,128]{1,0:T(8,128)S(1)}, f32[16,8,128]{2,1,0:T(8,128)S(1)}) custom-call(s32[6,4,8]{2,1,0:T(4,128)S(1)} %bitcast.9, s32[6,4,8]{2,1,0:T(4,128)S(1)} %bitcast.11, s32[8,6]{1,0:T(8,128)S(1)} %copy-done.7, s32[8]{0:T(128)S(1)} %copy-done.9, f32[3,128]{1,0:T(4,128)S(1)} %copy-done.8, ...), custom_call_target="tpu_custom_call" | custom-call | tf_op jit(solution)/shard_map/pallas_call | solution.py:287
  31.7 4.3 %all-to-all-done.1.moments = f32[16,1,128]{2,1,0:T(1,128)S(1)} async-done(((f32[16,1,128]{2,1,0:T(1,128)}), f32[16,1,128]{2,1,0:T(1,128)S(1)}, u32[]{:S(2)}, u32[]{:S(2)}) %all-to-all-start.1) | async-done | bytes 8224 | tf_op jit(solution)/shard_map/all_to_all | solution.py:286
  36.0 1.0 %shard_map.110 = (f32[8,768]{1,0:T(8,128)S(1)}, bf16[16,7,8,128]{3,2,1,0:T(8,128)(2,1)S(1)}) custom-call(f32[16,1,128]{2,1,0:T(1,128)S(1)} %all-to-all-done.1.moments, f32[16,8,128]{2,1,0:T(8,128)S(1)} %get-tuple-element.12.weights, f32[6,8,128]{2,1,0:T(8,128)S(1)} %get-tuple-element.13.rest, f32[8,128]{1,0:T(8,128)S(1)} %get-tuple-element.14.live, ...), custom_call_target="tpu_custom_call" | custom-call | tf_op jit(solution)/shard_map/pallas_call | solution.py:311
  37.0 10.7 %all_to_all.21.received.own = bf16[16,7,8,128]{3,2,1,0:T(8,128)(2,1)S(1)} all-to-all(bf16[16,7,8,128]{3,2,1,0:T(8,128)(2,1)S(1)} %get-tuple-element.15), channel_id=1, replica_groups=mesh['bubble'=16,'panel'=16] {'panel'}, dimensions={0} | all-to-all | bytes 458752 | tf_op jit(solution)/shard_map/all_to_all | solution.py:275
  47.7 0.0 collective-permute-start.2
  47.7 1.2 %collective-permute-start.3 = (bf16[16,7,8,128]{3,2,1,0:T(8,128)(2,1)S(1)}, bf16[16,7,8,128]{3,2,1,0:T(8,128)(2,1)S(1)}, u32[]{:S(2)}, u32[]{:S(2)}) collective-permute-start(bf16[16,7,8,128]{3,2,1,0:T(8,128)(2,1)S(1)} %all_to_all.21.received.own), channel_id=1, source_target_pairs={{0,16},{16,0},{32,48},{48,32},{64,80},{80,64},{96,112},{112,96},{1... | collective-permute-start | bytes 688136 | tf_op jit(solution)/shard_map/ppermute | solution.py:276
  48.9 0.6 moments.3
  49.5 7.3 %all-to-all-start.3 = ((f32[16,1,128]{2,1,0:T(1,128)}), f32[16,1,128]{2,1,0:T(1,128)S(1)}, u32[]{:S(2)}, u32[]{:S(2)}) async-start(f32[16,1,128]{2,1,0:T(1,128)} %moments.3), calls=%async_computation.3 | async-start | bytes 16384 | tf_op jit(solution)/shard_map/all_to_all | solution.py:286
  56.8 2.2 %collective-permute-done.2.odd_swap = bf16[16,7,8,128]{3,2,1,0:T(8,128)(2,1)S(1)} collective-permute-done((bf16[16,7,8,128]{3,2,1,0:T(8,128)(2,1)S(1)}, bf16[16,7,8,128]{3,2,1,0:T(8,128)(2,1)S(1)}, u32[]{:S(2)}, u32[]{:S(2)}) %collective-permute-start.2) | collective-permute-done | bytes 229408 | tf_op jit(solution)/shard_map/ppermute | solution.py:277
  59.0 3.5 %shard_map.111 = (f32[6,8,128]{2,1,0:T(8,128)S(1)}, f32[8,128]{1,0:T(8,128)S(1)}) custom-call(s32[6,4,8]{2,1,0:T(4,128)S(1)} %bitcast.10, s32[6,4,8]{2,1,0:T(4,128)S(1)} %bitcast.12, s32[8,6]{1,0:T(8,128)S(1)} %copy-done.7, s32[8]{0:T(128)S(1)} %copy-done.9, f32[3,128]{1,0:T(4,128)S(1)} %copy-done.8, ...), custom_call_target="tpu_custom_call" | custom-call | tf_op jit(solution)/shard_map/pallas_call | solution.py:287
  62.5 4.2 %all-to-all-done.3.moments = f32[16,1,128]{2,1,0:T(1,128)S(1)} async-done(((f32[16,1,128]{2,1,0:T(1,128)}), f32[16,1,128]{2,1,0:T(1,128)S(1)}, u32[]{:S(2)}, u32[]{:S(2)}) %all-to-all-start.3) | async-done | bytes 8224 | tf_op jit(solution)/shard_map/all_to_all | solution.py:286
  66.7 1.4 %shard_map.112 = f32[8,768]{1,0:T(8,128)} custom-call(f32[16,1,128]{2,1,0:T(1,128)S(1)} %all-to-all-done.3.moments, f32[16,8,128]{2,1,0:T(8,128)S(1)} %get-tuple-element.12.weights, f32[6,8,128]{2,1,0:T(8,128)S(1)} %get-tuple-element.16.rest, f32[8,128]{1,0:T(8,128)S(1)} %get-tuple-element.17.live, bf16[128,768]{1,0:T(8,128)(2,1)S(1)} %bitcast.8, ...), custom_call_target="tpu_custom_call" | custom-call | tf_op jit(solution)/shard_map/pallas_call | solution.py:311
  (17 shorter events, 0.0 us)
Async XLA Ops:
  0.0 28.1 %copy-start.3 = (f32[8,768]{1,0:T(8,128)S(1)}, f32[8,768]{1,0:T(8,128)}, u32[]{:S(2)}) copy-start(f32[8,768]{1,0:T(8,128)} %right_side.3) | copy-start | bytes 73732
  0.0 28.1 %copy-start.4 = (s32[8,6,4]{0,2,1:T(4,128)S(1)}, s32[8,6,4]{0,2,1:T(4,128)}, u32[]{:S(2)}) copy-start(s32[8,6,4]{0,2,1:T(4,128)} %param.15) | copy-start | bytes 2308
  0.0 28.1 %copy-start.5 = (s32[8,6,4]{0,2,1:T(4,128)S(1)}, s32[8,6,4]{0,2,1:T(4,128)}, u32[]{:S(2)}) copy-start(s32[8,6,4]{0,2,1:T(4,128)} %param.16) | copy-start | bytes 2308
  0.0 28.1 %copy-start.7 = (s32[8,6]{1,0:T(8,128)S(1)}, s32[8,6]{1,0:T(8,128)}, u32[]{:S(2)}) copy-start(s32[8,6]{1,0:T(8,128)} %near_count.3) | copy-start | bytes 580
  0.0 28.1 %copy-start.8 = (f32[3,128]{1,0:T(4,128)S(1)}, f32[3,128]{1,0:T(4,128)}, u32[]{:S(2)}) copy-start(f32[3,128]{1,0:T(4,128)} %centres.3) | copy-start | bytes 4612
  0.0 28.1 %copy-start.9 = (s32[8]{0:T(128)S(1)}, s32[8]{0:T(128)}, u32[]{:S(2)}) copy-start(s32[8]{0:T(128)} %colour.3) | copy-start | bytes 100
  1.2 34.8 %copy-start = (bf16[8,6,128,128]{3,2,1,0:T(8,128)(2,1)S(1)}, bf16[8,6,128,128]{3,2,1,0:T(8,128)(2,1)}, u32[]{:S(2)}) copy-start(bf16[8,6,128,128]{3,2,1,0:T(8,128)(2,1)} %inv_diag.3) | copy-start | bytes 4718596
  1.3 34.8 %copy-start.1 = (bf16[8,16,768]{2,1,0:T(8,128)(2,1)S(1)}, bf16[8,16,768]{2,1,0:T(8,128)(2,1)}, u32[]{:S(2)}) copy-start(bf16[8,16,768]{2,1,0:T(8,128)(2,1)} %param.19) | copy-start | bytes 589828
  1.3 34.8 %copy-start.2 = (bf16[8,16,768]{2,1,0:T(8,128)(2,1)S(1)}, bf16[8,16,768]{2,1,0:T(8,128)(2,1)}, u32[]{:S(2)}) copy-start(bf16[8,16,768]{2,1,0:T(8,128)(2,1)} %param.20) | copy-start | bytes 589828
  1.3 34.8 %copy-start.6 = (f32[8,768]{1,0:T(8,128)S(1)}, f32[8,768]{1,0:T(8,128)}, u32[]{:S(2)}) copy-start(f32[8,768]{1,0:T(8,128)} %relaxed.1) | copy-start | bytes 73732
  13.1 13.5 %collective-permute-start = (bf16[16,7,8,128]{3,2,1,0:T(8,128)(2,1)S(1)}, bf16[16,7,8,128]{3,2,1,0:T(8,128)(2,1)S(1)}, u32[]{:S(2)}, u32[]{:S(2)}) collective-permute-start(bf16[16,7,8,128]{3,2,1,0:T(8,128)(2,1)S(1)} %all_to_all.20.received.own), channel_id=1, source_target_pairs={{16,32},{32,16},{48,64},{64,48},{80,96},{96,80},{112,128},{128,112... | collective-permute-start | bytes 688136 | tf_op jit(solution)/shard_map/ppermute | solution.py:277
  20.7 7.4 %collective-permute-start.1 = (bf16[16,7,8,128]{3,2,1,0:T(8,128)(2,1)S(1)}, bf16[16,7,8,128]{3,2,1,0:T(8,128)(2,1)S(1)}, u32[]{:S(2)}, u32[]{:S(2)}) collective-permute-start(bf16[16,7,8,128]{3,2,1,0:T(8,128)(2,1)S(1)} %all_to_all.20.received.own), channel_id=1, source_target_pairs={{0,16},{16,0},{32,48},{48,32},{64,80},{80,64},{96,112},{112,96},{1... | collective-permute-start | bytes 688136 | tf_op jit(solution)/shard_map/ppermute | solution.py:276
  21.4 14.7 %all-to-all-start.1 = ((f32[16,1,128]{2,1,0:T(1,128)}), f32[16,1,128]{2,1,0:T(1,128)S(1)}, u32[]{:S(2)}, u32[]{:S(2)}) async-start(f32[16,1,128]{2,1,0:T(1,128)} %moments.2), calls=%async_computation.1 | async-start | bytes 16384 | tf_op jit(solution)/shard_map/all_to_all | solution.py:286
  47.7 11.3 %collective-permute-start.2 = (bf16[16,7,8,128]{3,2,1,0:T(8,128)(2,1)S(1)}, bf16[16,7,8,128]{3,2,1,0:T(8,128)(2,1)S(1)}, u32[]{:S(2)}, u32[]{:S(2)}) collective-permute-start(bf16[16,7,8,128]{3,2,1,0:T(8,128)(2,1)S(1)} %all_to_all.21.received.own), channel_id=1, source_target_pairs={{16,32},{32,16},{48,64},{64,48},{80,96},{96,80},{112,128},{128,112... | collective-permute-start | bytes 688136 | tf_op jit(solution)/shard_map/ppermute | solution.py:277
  47.7 11.3 %collective-permute-start.3 = (bf16[16,7,8,128]{3,2,1,0:T(8,128)(2,1)S(1)}, bf16[16,7,8,128]{3,2,1,0:T(8,128)(2,1)S(1)}, u32[]{:S(2)}, u32[]{:S(2)}) collective-permute-start(bf16[16,7,8,128]{3,2,1,0:T(8,128)(2,1)S(1)} %all_to_all.21.received.own), channel_id=1, source_target_pairs={{0,16},{16,0},{32,48},{48,32},{64,80},{80,64},{96,112},{112,96},{1... | collective-permute-start | bytes 688136 | tf_op jit(solution)/shard_map/ppermute | solution.py:276
  49.5 17.2 %all-to-all-start.3 = ((f32[16,1,128]{2,1,0:T(1,128)}), f32[16,1,128]{2,1,0:T(1,128)S(1)}, u32[]{:S(2)}, u32[]{:S(2)}) async-start(f32[16,1,128]{2,1,0:T(1,128)} %moments.3), calls=%async_computation.3 | async-start | bytes 16384 | tf_op jit(solution)/shard_map/all_to_all | solution.py:286
where the time goes:
time: 68.5 us; the launch traced here: 68.2 us
  blocking collectives  22.5 us (33%)
  starting transfers between devices  20.8 us (30%)
  waiting for transfers between devices  12.7 us (19%)
  Pallas kernels  11.9 us (17%)
    all_to_all x2, blocking collectives, per_device(): received = lax.all_to_all(message, 'panel', 0, 0, tiled=True)  22.5 us
    all_to_all x2, starting transfers between devices, per_device(): moments = lax.all_to_all(own_moments, 'bubble', 0, 0, tiled=True)  12 us
    all_to_all x2, waiting for transfers between devices, per_device(): moments = lax.all_to_all(own_moments, 'bubble', 0, 0, tiled=True)  8.58 us
    ppermute x2, starting transfers between devices, per_device(): odd_swap = lax.ppermute(received, 'bubble', odd_pairs)  7.6 us
    pallas_call x2, Pallas kernels, per_device(): pl.pallas_call(functools.partial(near_kernel, colour_now), out_shape=near...  7.02 us
    ppermute x2, waiting for transfers between devices, per_device(): odd_swap = lax.ppermute(received, 'bubble', odd_pairs)  2.66 us
    pallas_call x2, Pallas kernels, per_device(): pl.pallas_call(functools.partial(finish_kernel, last), out_shape=[relaxed...  2.42 us
    ppermute x2, waiting for transfers between devices, per_device(): even_swap = lax.ppermute(received, 'bubble', even_pairs)  1.51 us
  transfers between devices with their start and end apart: 6, of which 5 were waited for; matrix products, arithmetic and copies ran while one was open for 0% of the time, Pallas kernels for 12%

commit v1 on v0

--- a/solution.py
+++ b/solution.py
@@ -89,9 +89,9 @@
     near_count,
     colour,
     centres,
-    odd_swap,
+    fetched,
     own,
-    even_swap,
+    traded,
     right_side,
     near_vals,
     rest,
@@ -103,7 +103,7 @@
     peers = own.shape[0]
     my_index = lax.axis_index("bubble")
     first = my_index * bub
-    even = (my_index & 1) == 0
+    in_order = (my_index & 1) == (lax.axis_index("panel") & 1) ^ 1
     none = 3 * peers * nblk * bub
 
     def copy(b):
@@ -116,7 +116,7 @@
             copy(b).start()
 
     rows = row_ids((bub, blk))
-    for o, ref in enumerate((odd_swap, own, even_swap)):
+    for o, ref in enumerate((fetched, own, traded)):
         for p in range(peers):
             for j in range(nblk):
                 at = ((o * peers + p) * nblk + j) * bub
@@ -144,7 +144,7 @@
                 for s in range(slots):
                     local = near_bubble[r, s, b] - (first - bub)
                     o = local >> shift_of(bub)
-                    o = jnp.where(even, o, 2 - o)
+                    o = jnp.where(in_order, o, 2 - o)
                     row = (o * peers * nblk + near_block[r, s, b]) * bub + (local & (bub - 1))
                     i = jnp.where(s < near_count[b, r], row, none)
                     picked.append(jnp.where(here, sources[pl.ds(i, 1), :], 0.0))
@@ -247,10 +247,12 @@
         jax.ShapeDtypeStruct((groups, bub, blk), jnp.float32),
     ]
     relaxed_shape = jax.ShapeDtypeStruct((bub, panels), jnp.float32)
-    pairs = [(i, i + 1) for i in range(groups - 1)]
-    odd_pairs = [(i, j) for p in pairs[1::2] for i, j in (p, p[::-1])]
-    odd_pairs += [(0, groups - 1), (groups - 1, 0)]
-    even_pairs = [(i, j) for p in pairs[0::2] for i, j in (p, p[::-1])]
+    fetch = []
+    for g in range(groups):
+        for p in range(peers):
+            other = g ^ 1 if p % 2 == 0 else ((g + 1) ^ 1) - 1
+            fetch.append((g * peers + p, other % groups * peers + p))
+    trade = [(p, p ^ 1) for p in range(peers)]
 
     message = pl.pallas_call(
         first_kernel,
@@ -273,8 +275,8 @@
     for colour_now in range(2):
         last = colour_now == 1
         received = lax.all_to_all(message, "panel", 0, 0, tiled=True)
-        even_swap = lax.ppermute(received, "bubble", even_pairs)
-        odd_swap = lax.ppermute(received, "bubble", odd_pairs)
+        fetched = lax.ppermute(received, ("bubble", "panel"), fetch)
+        traded = lax.ppermute(fetched, "panel", trade)
         own_moments = pl.pallas_call(
             moment_kernel,
             out_shape=jax.ShapeDtypeStruct((groups, 1, blk), jnp.float32),
@@ -301,9 +303,9 @@
             near_count,
             colour,
             centres,
-            odd_swap,
+            fetched,
             received,
-            even_swap,
+            traded,
             right_side,
             near_vals,
         )

time: 68.5 us -> 77.6 us (1.13)
  waiting for transfers between devices: 12.7 us -> 22.2 us
    ppermute x4, waiting for transfers between devices: 4.17 us -> 9.54 us  [the longest x2 9.53 us: per_device(): fetched = lax.ppermute(received, ('bubble', 'panel'), fetch)]
    all_to_all x2, waiting for transfers between devices: 8.58 us -> 12.7 us  [per_device(): moments = lax.all_to_all(own_moments, 'bubble', 0, 0, tiled=True)]
    all_to_all x2, starting transfers between devices: 12 us -> 10.2 us  [per_device(): moments = lax.all_to_all(own_moments, 'bubble', 0, 0, tiled=True)]
    ppermute x4, starting transfers between devices: 8.77 us -> 9.9 us  [the longest x2 7.39 us: per_device(): traded = lax.ppermute(fetched, 'panel', trade)]
  transfers between devices with their start and end apart: 6 -> 6, of which waited for: 5 -> 4; matrix products, arithmetic and copies ran while one was open for 0% -> 0% of each run, Pallas kernels for 12% -> 11%
where the time goes in v1:
time: 77.6 us; the launch traced here: 76.7 us
  blocking collectives  22.3 us (29%)
  waiting for transfers between devices  22.2 us (29%)
  starting transfers between devices  20.1 us (26%)
  Pallas kernels  11.9 us (15%)
    all_to_all x2, blocking collectives, per_device(): received = lax.all_to_all(message, 'panel', 0, 0, tiled=True)  22.3 us
    all_to_all x2, waiting for transfers between devices, per_device(): moments = lax.all_to_all(own_moments, 'bubble', 0, 0, tiled=True)  12.7 us
    all_to_all x2, starting transfers between devices, per_device(): moments = lax.all_to_all(own_moments, 'bubble', 0, 0, tiled=True)  10.2 us
    ppermute x2, waiting for transfers between devices, per_device(): fetched = lax.ppermute(received, ('bubble', 'panel'), fetch)  9.53 us
    ppermute x2, starting transfers between devices, per_device(): traded = lax.ppermute(fetched, 'panel', trade)  7.39 us
    pallas_call x2, Pallas kernels, per_device(): pl.pallas_call(functools.partial(near_kernel, colour_now), out_shape=near...  7.03 us
    ppermute x2, starting transfers between devices, per_device(): fetched = lax.ppermute(received, ('bubble', 'panel'), fetch)  2.51 us
    pallas_call x2, Pallas kernels, per_device(): pl.pallas_call(functools.partial(finish_kernel, last), out_shape=[relaxed...  2.42 us
  transfers between devices with their start and end apart: 6, of which 4 were waited for; matrix products, arithmetic and copies ran while one was open for 0% of the time, Pallas kernels for 11%

profile of v1, /device:TPU:8, one launch (start us, length us, event | category | flops | bytes accessed | tf_op | source)
XLA Modules:
  0.0 76.7 jit_solution(8963257751442748234)
XLA Ops:
  0.0 1.2 %first.1 = bf16[16,7,8,128]{3,2,1,0:T(8,128)(2,1)S(1)} custom-call(f32[8,768]{1,0:T(8,128)} %relaxed.1, bf16[128,768]{1,0:T(8,128)(2,1)} %bitcast.4), custom_call_target="tpu_custom_call" | custom-call | flops 17179869184 | bytes 1048576 | tf_op jit(solution)/shard_map/first/pallas_call | solution.py:257
  1.2 0.0 copy-start
  1.3 0.0 copy-start.1
  1.3 0.0 copy-start.2
  1.3 0.0 copy-start.6
  1.3 11.8 %all_to_all.20.received.own = bf16[16,7,8,128]{3,2,1,0:T(8,128)(2,1)S(1)} all-to-all(bf16[16,7,8,128]{3,2,1,0:T(8,128)(2,1)S(1)} %first.1), channel_id=1, replica_groups=mesh['bubble'=16,'panel'=16] {'panel'}, dimensions={0} | all-to-all | bytes 458752 | tf_op jit(solution)/shard_map/all_to_all | solution.py:277
  13.1 1.9 %collective-permute-start = (bf16[16,7,8,128]{3,2,1,0:T(8,128)(2,1)S(1)}, bf16[16,7,8,128]{3,2,1,0:T(8,128)(2,1)S(1)}, u32[]{:S(2)}, u32[]{:S(2)}) collective-permute-start(bf16[16,7,8,128]{3,2,1,0:T(8,128)(2,1)S(1)} %all_to_all.20.received.own), channel_id=1, source_target_pairs={{0,16},{1,241},{2,18},{3,243},{4,20},{5,245},{6,22},{7,247},{8,24}... | collective-permute-start | bytes 688136 | tf_op jit(solution)/shard_map/ppermute | solution.py:278
  15.1 4.1 %collective-permute-done.fetched = bf16[16,7,8,128]{3,2,1,0:T(8,128)(2,1)S(1)} collective-permute-done((bf16[16,7,8,128]{3,2,1,0:T(8,128)(2,1)S(1)}, bf16[16,7,8,128]{3,2,1,0:T(8,128)(2,1)S(1)}, u32[]{:S(2)}, u32[]{:S(2)}) %collective-permute-start) | collective-permute-done | bytes 229408 | tf_op jit(solution)/shard_map/ppermute | solution.py:278
  19.2 4.8 %collective-permute-start.1 = (bf16[16,7,8,128]{3,2,1,0:T(8,128)(2,1)S(1)}, bf16[16,7,8,128]{3,2,1,0:T(8,128)(2,1)S(1)}, u32[]{:S(2)}, u32[]{:S(2)}) collective-permute-start(bf16[16,7,8,128]{3,2,1,0:T(8,128)(2,1)S(1)} %collective-permute-done.fetched), channel_id=1, source_target_pairs={{0,1},{1,0},{2,3},{3,2},{4,5},{5,4},{6,7},{7,6},{8,9},{9,8},{10,11... | collective-permute-start | bytes 688136 | tf_op jit(solution)/shard_map/ppermute | solution.py:279
  24.0 0.6 moments.2
  24.6 6.7 %all-to-all-start.1 = ((f32[16,1,128]{2,1,0:T(1,128)}), f32[16,1,128]{2,1,0:T(1,128)S(1)}, u32[]{:S(2)}, u32[]{:S(2)}) async-start(f32[16,1,128]{2,1,0:T(1,128)} %moments.2), calls=%async_computation.1 | async-start | bytes 16384 | tf_op jit(solution)/shard_map/all_to_all | solution.py:288
  31.3 0.0 collective-permute-done.1.traded
  31.4 3.5 %shard_map.109 = (f32[6,8,128]{2,1,0:T(8,128)S(1)}, f32[8,128]{1,0:T(8,128)S(1)}, f32[16,8,128]{2,1,0:T(8,128)S(1)}) custom-call(s32[6,4,8]{2,1,0:T(4,128)S(1)} %bitcast.9, s32[6,4,8]{2,1,0:T(4,128)S(1)} %bitcast.11, s32[8,6]{1,0:T(8,128)S(1)} %copy-done.7, s32[8]{0:T(128)S(1)} %copy-done.9, f32[3,128]{1,0:T(4,128)S(1)} %copy-done.8, ...), custom_call_target="tpu_custom_call" | custom-call | tf_op jit(solution)/shard_map/pallas_call | solution.py:289
  34.9 6.3 %all-to-all-done.1.moments = f32[16,1,128]{2,1,0:T(1,128)S(1)} async-done(((f32[16,1,128]{2,1,0:T(1,128)}), f32[16,1,128]{2,1,0:T(1,128)S(1)}, u32[]{:S(2)}, u32[]{:S(2)}) %all-to-all-start.1) | async-done | bytes 8224 | tf_op jit(solution)/shard_map/all_to_all | solution.py:288
  41.3 1.0 %shard_map.110 = (f32[8,768]{1,0:T(8,128)S(1)}, bf16[16,7,8,128]{3,2,1,0:T(8,128)(2,1)S(1)}) custom-call(f32[16,1,128]{2,1,0:T(1,128)S(1)} %all-to-all-done.1.moments, f32[16,8,128]{2,1,0:T(8,128)S(1)} %get-tuple-element.12.weights, f32[6,8,128]{2,1,0:T(8,128)S(1)} %get-tuple-element.13.rest, f32[8,128]{1,0:T(8,128)S(1)} %get-tuple-element.14.live, ...), custom_call_target="tpu_custom_call" | custom-call | tf_op jit(solution)/shard_map/pallas_call | solution.py:313
  42.3 10.5 %all_to_all.21.received.own = bf16[16,7,8,128]{3,2,1,0:T(8,128)(2,1)S(1)} all-to-all(bf16[16,7,8,128]{3,2,1,0:T(8,128)(2,1)S(1)} %get-tuple-element.15), channel_id=1, replica_groups=mesh['bubble'=16,'panel'=16] {'panel'}, dimensions={0} | all-to-all | bytes 458752 | tf_op jit(solution)/shard_map/all_to_all | solution.py:277
  52.7 0.6 collective-permute-start.2
  53.3 5.4 %collective-permute-done.2.fetched = bf16[16,7,8,128]{3,2,1,0:T(8,128)(2,1)S(1)} collective-permute-done((bf16[16,7,8,128]{3,2,1,0:T(8,128)(2,1)S(1)}, bf16[16,7,8,128]{3,2,1,0:T(8,128)(2,1)S(1)}, u32[]{:S(2)}, u32[]{:S(2)}) %collective-permute-start.2) | collective-permute-done | bytes 229408 | tf_op jit(solution)/shard_map/ppermute | solution.py:278
  58.8 2.6 %collective-permute-start.3 = (bf16[16,7,8,128]{3,2,1,0:T(8,128)(2,1)S(1)}, bf16[16,7,8,128]{3,2,1,0:T(8,128)(2,1)S(1)}, u32[]{:S(2)}, u32[]{:S(2)}) collective-permute-start(bf16[16,7,8,128]{3,2,1,0:T(8,128)(2,1)S(1)} %collective-permute-done.2.fetched), channel_id=1, source_target_pairs={{0,1},{1,0},{2,3},{3,2},{4,5},{5,4},{6,7},{7,6},{8,9},{9,8},{10,11... | collective-permute-start | bytes 688136 | tf_op jit(solution)/shard_map/ppermute | solution.py:279
  61.3 0.6 moments.3
  62.0 3.5 %all-to-all-start.3 = ((f32[16,1,128]{2,1,0:T(1,128)}), f32[16,1,128]{2,1,0:T(1,128)S(1)}, u32[]{:S(2)}, u32[]{:S(2)}) async-start(f32[16,1,128]{2,1,0:T(1,128)} %moments.3), calls=%async_computation.3 | async-start | bytes 16384 | tf_op jit(solution)/shard_map/all_to_all | solution.py:288
  65.5 3.5 %shard_map.111 = (f32[6,8,128]{2,1,0:T(8,128)S(1)}, f32[8,128]{1,0:T(8,128)S(1)}) custom-call(s32[6,4,8]{2,1,0:T(4,128)S(1)} %bitcast.10, s32[6,4,8]{2,1,0:T(4,128)S(1)} %bitcast.12, s32[8,6]{1,0:T(8,128)S(1)} %copy-done.7, s32[8]{0:T(128)S(1)} %copy-done.9, f32[3,128]{1,0:T(4,128)S(1)} %copy-done.8, ...), custom_call_target="tpu_custom_call" | custom-call | tf_op jit(solution)/shard_map/pallas_call | solution.py:289
  69.0 6.3 %all-to-all-done.3.moments = f32[16,1,128]{2,1,0:T(1,128)S(1)} async-done(((f32[16,1,128]{2,1,0:T(1,128)}), f32[16,1,128]{2,1,0:T(1,128)S(1)}, u32[]{:S(2)}, u32[]{:S(2)}) %all-to-all-start.3) | async-done | bytes 8224 | tf_op jit(solution)/shard_map/all_to_all | solution.py:288
  75.3 1.4 %shard_map.112 = f32[8,768]{1,0:T(8,128)} custom-call(f32[16,1,128]{2,1,0:T(1,128)S(1)} %all-to-all-done.3.moments, f32[16,8,128]{2,1,0:T(8,128)S(1)} %get-tuple-element.12.weights, f32[6,8,128]{2,1,0:T(8,128)S(1)} %get-tuple-element.16.rest, f32[8,128]{1,0:T(8,128)S(1)} %get-tuple-element.17.live, bf16[128,768]{1,0:T(8,128)(2,1)S(1)} %bitcast.8, ...), custom_call_target="tpu_custom_call" | custom-call | tf_op jit(solution)/shard_map/pallas_call | solution.py:313
  (17 shorter events, 0.0 us)
Async XLA Ops:
  0.0 31.4 %copy-start.3 = (f32[8,768]{1,0:T(8,128)S(1)}, f32[8,768]{1,0:T(8,128)}, u32[]{:S(2)}) copy-start(f32[8,768]{1,0:T(8,128)} %right_side.3) | copy-start | bytes 73732
  0.0 31.4 %copy-start.4 = (s32[8,6,4]{0,2,1:T(4,128)S(1)}, s32[8,6,4]{0,2,1:T(4,128)}, u32[]{:S(2)}) copy-start(s32[8,6,4]{0,2,1:T(4,128)} %param.15) | copy-start | bytes 2308
  0.0 31.4 %copy-start.5 = (s32[8,6,4]{0,2,1:T(4,128)S(1)}, s32[8,6,4]{0,2,1:T(4,128)}, u32[]{:S(2)}) copy-start(s32[8,6,4]{0,2,1:T(4,128)} %param.16) | copy-start | bytes 2308
  0.0 31.4 %copy-start.7 = (s32[8,6]{1,0:T(8,128)S(1)}, s32[8,6]{1,0:T(8,128)}, u32[]{:S(2)}) copy-start(s32[8,6]{1,0:T(8,128)} %near_count.3) | copy-start | bytes 580
  0.0 31.4 %copy-start.8 = (f32[3,128]{1,0:T(4,128)S(1)}, f32[3,128]{1,0:T(4,128)}, u32[]{:S(2)}) copy-start(f32[3,128]{1,0:T(4,128)} %centres.3) | copy-start | bytes 4612
  0.0 31.4 %copy-start.9 = (s32[8]{0:T(128)S(1)}, s32[8]{0:T(128)}, u32[]{:S(2)}) copy-start(s32[8]{0:T(128)} %colour.3) | copy-start | bytes 100
  1.2 40.0 %copy-start = (bf16[8,6,128,128]{3,2,1,0:T(8,128)(2,1)S(1)}, bf16[8,6,128,128]{3,2,1,0:T(8,128)(2,1)}, u32[]{:S(2)}) copy-start(bf16[8,6,128,128]{3,2,1,0:T(8,128)(2,1)} %inv_diag.3) | copy-start | bytes 4718596
  1.3 40.0 %copy-start.1 = (bf16[8,16,768]{2,1,0:T(8,128)(2,1)S(1)}, bf16[8,16,768]{2,1,0:T(8,128)(2,1)}, u32[]{:S(2)}) copy-start(bf16[8,16,768]{2,1,0:T(8,128)(2,1)} %param.19) | copy-start | bytes 589828
  1.3 40.0 %copy-start.2 = (bf16[8,16,768]{2,1,0:T(8,128)(2,1)S(1)}, bf16[8,16,768]{2,1,0:T(8,128)(2,1)}, u32[]{:S(2)}) copy-start(bf16[8,16,768]{2,1,0:T(8,128)(2,1)} %param.20) | copy-start | bytes 589828
  1.3 40.0 %copy-start.6 = (f32[8,768]{1,0:T(8,128)S(1)}, f32[8,768]{1,0:T(8,128)}, u32[]{:S(2)}) copy-start(f32[8,768]{1,0:T(8,128)} %relaxed.1) | copy-start | bytes 73732
  13.1 6.0 %collective-permute-start = (bf16[16,7,8,128]{3,2,1,0:T(8,128)(2,1)S(1)}, bf16[16,7,8,128]{3,2,1,0:T(8,128)(2,1)S(1)}, u32[]{:S(2)}, u32[]{:S(2)}) collective-permute-start(bf16[16,7,8,128]{3,2,1,0:T(8,128)(2,1)S(1)} %all_to_all.20.received.own), channel_id=1, source_target_pairs={{0,16},{1,241},{2,18},{3,243},{4,20},{5,245},{6,22},{7,247},{8,24}... | collective-permute-start | bytes 688136 | tf_op jit(solution)/shard_map/ppermute | solution.py:278
  19.2 12.2 %collective-permute-start.1 = (bf16[16,7,8,128]{3,2,1,0:T(8,128)(2,1)S(1)}, bf16[16,7,8,128]{3,2,1,0:T(8,128)(2,1)S(1)}, u32[]{:S(2)}, u32[]{:S(2)}) collective-permute-start(bf16[16,7,8,128]{3,2,1,0:T(8,128)(2,1)S(1)} %collective-permute-done.fetched), channel_id=1, source_target_pairs={{0,1},{1,0},{2,3},{3,2},{4,5},{5,4},{6,7},{7,6},{8,9},{9,8},{10,11... | collective-permute-start | bytes 688136 | tf_op jit(solution)/shard_map/ppermute | solution.py:279
  24.6 16.7 %all-to-all-start.1 = ((f32[16,1,128]{2,1,0:T(1,128)}), f32[16,1,128]{2,1,0:T(1,128)S(1)}, u32[]{:S(2)}, u32[]{:S(2)}) async-start(f32[16,1,128]{2,1,0:T(1,128)} %moments.2), calls=%async_computation.1 | async-start | bytes 16384 | tf_op jit(solution)/shard_map/all_to_all | solution.py:288
  52.7 6.0 %collective-permute-start.2 = (bf16[16,7,8,128]{3,2,1,0:T(8,128)(2,1)S(1)}, bf16[16,7,8,128]{3,2,1,0:T(8,128)(2,1)S(1)}, u32[]{:S(2)}, u32[]{:S(2)}) collective-permute-start(bf16[16,7,8,128]{3,2,1,0:T(8,128)(2,1)S(1)} %all_to_all.21.received.own), channel_id=1, source_target_pairs={{0,16},{1,241},{2,18},{3,243},{4,20},{5,245},{6,22},{7,247},{8,24}... | collective-permute-start | bytes 688136 | tf_op jit(solution)/shard_map/ppermute | solution.py:278
  58.8 6.7 %collective-permute-start.3 = (bf16[16,7,8,128]{3,2,1,0:T(8,128)(2,1)S(1)}, bf16[16,7,8,128]{3,2,1,0:T(8,128)(2,1)S(1)}, u32[]{:S(2)}, u32[]{:S(2)}) collective-permute-start(bf16[16,7,8,128]{3,2,1,0:T(8,128)(2,1)S(1)} %collective-permute-done.2.fetched), channel_id=1, source_target_pairs={{0,1},{1,0},{2,3},{3,2},{4,5},{5,4},{6,7},{7,6},{8,9},{9,8},{10,11... | collective-permute-start | bytes 688136 | tf_op jit(solution)/shard_map/ppermute | solution.py:279
  62.0 13.3 %all-to-all-start.3 = ((f32[16,1,128]{2,1,0:T(1,128)}), f32[16,1,128]{2,1,0:T(1,128)S(1)}, u32[]{:S(2)}, u32[]{:S(2)}) async-start(f32[16,1,128]{2,1,0:T(1,128)} %moments.3), calls=%async_computation.3 | async-start | bytes 16384 | tf_op jit(solution)/shard_map/all_to_all | solution.py:288

commit v2 on v1

--- a/solution.py
+++ b/solution.py
@@ -84,10 +84,10 @@
 
 def near_kernel(
     colour_now,
-    near_bubble,
-    near_block,
-    near_count,
-    colour,
+    near_bubble_in,
+    near_block_in,
+    near_count_in,
+    colour_in,
     centres,
     fetched,
     own,
@@ -98,7 +98,21 @@
     live,
     *refs,
 ):
-    *weights, sources, vals, sems = refs
+    *weights, sources, vals, near_bubble, near_block, near_count, colour, table_sems, sems = refs
+    tables = [
+        pltpu.make_async_copy(src, dst, table_sems.at[n])
+        for n, (src, dst) in enumerate(
+            (
+                (colour_in, colour),
+                (near_bubble_in, near_bubble),
+                (near_block_in, near_block),
+                (near_count_in, near_count),
+            )
+        )
+    ]
+    for t in tables:
+        t.start()
+    tables[0].wait()
     bub, nblk, slots, blk, _ = near_vals.shape
     peers = own.shape[0]
     my_index = lax.axis_index("bubble")
@@ -133,6 +147,9 @@
         lane = lax.broadcasted_iota(jnp.int32, (bub, blk), 1)
         for q in range(table.shape[0]):
             table[q] = jnp.take_along_axis(weight, q * bub + lane // (blk // bub), axis=1)
+
+    for t in tables[1:]:
+        t.wait()
 
     def near_of(b, carry):
         @pl.when(colour[b] == colour_now)
@@ -251,7 +268,10 @@
     for g in range(groups):
         for p in range(peers):
             other = g ^ 1 if p % 2 == 0 else ((g + 1) ^ 1) - 1
-            fetch.append((g * peers + p, other % groups * peers + p))
+            if 0 <= other < groups:
+                fetch.append((g * peers + p, other * peers + p))
+            else:
+                fetch.append((g * peers + p, g * peers + (p ^ 2)))
     trade = [(p, p ^ 1) for p in range(peers)]
 
     message = pl.pallas_call(
@@ -289,11 +309,16 @@
         rest, live, *table = pl.pallas_call(
             functools.partial(near_kernel, colour_now),
             out_shape=near_shapes[: 2 if last else 3],
-            in_specs=[SMEM] * 4 + [VMEM] * 5 + [HBM],
+            in_specs=[VMEM] * 9 + [HBM],
             out_specs=[VMEM] * (2 if last else 3),
             scratch_shapes=[
                 pltpu.VMEM(((3 * peers * nblk + 1) * bub, blk), jnp.float32),
                 pltpu.VMEM((bub, nblk, slots, blk, blk), jnp.bfloat16),
+                pltpu.SMEM((nblk, slots, bub), jnp.int32),
+                pltpu.SMEM((nblk, slots, bub), jnp.int32),
+                pltpu.SMEM((bub, nblk), jnp.int32),
+                pltpu.SMEM((bub,), jnp.int32),
+                pltpu.SemaphoreType.DMA((4,)),
                 pltpu.SemaphoreType.DMA((bub,)),
             ],
             compiler_params=limit(12),

time: 77.6 us -> 74.9 us (0.965)
  starting transfers between devices: 20.1 us -> 17.6 us
  waiting for transfers between devices: 22.2 us -> 23.1 us
  Pallas kernels: 11.9 us -> 11 us
    ppermute x2, starting transfers between devices: 7.39 us -> 0.01 us  [per_device(): traded = lax.ppermute(fetched, 'panel', trade)]
    all_to_all x2, starting transfers between devices: 10.2 us -> 15.1 us  [per_device(): moments = lax.all_to_all(own_moments, 'bubble', 0, 0, tiled=True)]
    all_to_all x2, waiting for transfers between devices: 12.7 us -> 13.6 us  [per_device(): moments = lax.all_to_all(own_moments, 'bubble', 0, 0, tiled=True)]
    pallas_call x2, Pallas kernels: 7.03 us -> 6.16 us  [per_device(): pl.pallas_call(functools.partial(near_kernel, colour_now), out_shape=near...]
  transfers between devices with their start and end apart: 6 -> 6, of which waited for: 4 -> 4; matrix products, arithmetic and copies ran while one was open for 0% -> 0% of each run, Pallas kernels for 11% -> 10%
where the time goes in v2:
time: 74.9 us; the launch traced here: 74.3 us
  waiting for transfers between devices  23.1 us (31%)
  blocking collectives  22.3 us (30%)
  starting transfers between devices  17.6 us (23%)
  Pallas kernels  11 us (15%)
    all_to_all x2, blocking collectives, per_device(): received = lax.all_to_all(message, 'panel', 0, 0, tiled=True)  22.3 us
    all_to_all x2, starting transfers between devices, per_device(): moments = lax.all_to_all(own_moments, 'bubble', 0, 0, tiled=True)  15.1 us
    all_to_all x2, waiting for transfers between devices, per_device(): moments = lax.all_to_all(own_moments, 'bubble', 0, 0, tiled=True)  13.6 us
    ppermute x2, waiting for transfers between devices, per_device(): fetched = lax.ppermute(received, ('bubble', 'panel'), fetch)  9.52 us
    pallas_call x2, Pallas kernels, per_device(): pl.pallas_call(functools.partial(near_kernel, colour_now), out_shape=near...  6.16 us
    ppermute x2, starting transfers between devices, per_device(): fetched = lax.ppermute(received, ('bubble', 'panel'), fetch)  2.52 us
    pallas_call x2, Pallas kernels, per_device(): pl.pallas_call(functools.partial(finish_kernel, last), out_shape=[relaxed...  2.42 us
  transfers between devices with their start and end apart: 6, of which 4 were waited for; matrix products, arithmetic and copies ran while one was open for 0% of the time, Pallas kernels for 10%

profile of v2, /device:TPU:8, one launch (start us, length us, event | category | flops | bytes accessed | tf_op | source)
XLA Modules:
  0.0 74.3 jit_solution(3979936843544596272)
XLA Ops:
  0.0 1.2 %first.1 = bf16[16,7,8,128]{3,2,1,0:T(8,128)(2,1)S(1)} custom-call(f32[8,768]{1,0:T(8,128)} %relaxed.1, bf16[128,768]{1,0:T(8,128)(2,1)} %bitcast.4), custom_call_target="tpu_custom_call" | custom-call | flops 17179869184 | bytes 1048576 | tf_op jit(solution)/shard_map/first/pallas_call | solution.py:277
  1.2 0.0 copy-start
  1.3 0.0 copy-start.1
  1.3 0.0 copy-start.2
  1.3 0.0 copy-start.6
  1.3 11.8 %all_to_all.20.received.own = bf16[16,7,8,128]{3,2,1,0:T(8,128)(2,1)S(1)} all-to-all(bf16[16,7,8,128]{3,2,1,0:T(8,128)(2,1)S(1)} %first.1), channel_id=1, replica_groups=mesh['bubble'=16,'panel'=16] {'panel'}, dimensions={0} | all-to-all | bytes 458752 | tf_op jit(solution)/shard_map/all_to_all | solution.py:297
  13.1 1.9 %collective-permute-start = (bf16[16,7,8,128]{3,2,1,0:T(8,128)(2,1)S(1)}, bf16[16,7,8,128]{3,2,1,0:T(8,128)(2,1)S(1)}, u32[]{:S(2)}, u32[]{:S(2)}) collective-permute-start(bf16[16,7,8,128]{3,2,1,0:T(8,128)(2,1)S(1)} %all_to_all.20.received.own), channel_id=1, source_target_pairs={{0,16},{1,3},{2,18},{3,1},{4,20},{5,7},{6,22},{7,5},{8,24},{9,11},... | collective-permute-start | bytes 688136 | tf_op jit(solution)/shard_map/ppermute | solution.py:298
  15.1 4.1 %collective-permute-done.fetched = bf16[16,7,8,128]{3,2,1,0:T(8,128)(2,1)S(1)} collective-permute-done((bf16[16,7,8,128]{3,2,1,0:T(8,128)(2,1)S(1)}, bf16[16,7,8,128]{3,2,1,0:T(8,128)(2,1)S(1)}, u32[]{:S(2)}, u32[]{:S(2)}) %collective-permute-start) | collective-permute-done | bytes 229408 | tf_op jit(solution)/shard_map/ppermute | solution.py:298
  19.2 0.0 collective-permute-start.1
  19.2 0.6 moments.2
  19.8 10.5 %all-to-all-start.1 = ((f32[16,1,128]{2,1,0:T(1,128)}), f32[16,1,128]{2,1,0:T(1,128)S(1)}, u32[]{:S(2)}, u32[]{:S(2)}) async-start(f32[16,1,128]{2,1,0:T(1,128)} %moments.2), calls=%async_computation.1 | async-start | bytes 16384 | tf_op jit(solution)/shard_map/all_to_all | solution.py:308
  30.3 3.1 %shard_map.109 = (f32[6,8,128]{2,1,0:T(8,128)S(1)}, f32[8,128]{1,0:T(8,128)S(1)}, f32[16,8,128]{2,1,0:T(8,128)S(1)}) custom-call(s32[6,4,8]{2,1,0:T(4,128)S(1)} %bitcast.9, s32[6,4,8]{2,1,0:T(4,128)S(1)} %bitcast.11, s32[8,6]{1,0:T(8,128)S(1)} %copy-done.7, s32[8]{0:T(128)S(1)} %copy-done.9, f32[3,128]{1,0:T(4,128)S(1)} %copy-done.8, ...), custom_call_target="tpu_custom_call" | custom-call | tf_op jit(solution)/shard_map/pallas_call | solution.py:309
  33.4 6.8 %all-to-all-done.1.moments = f32[16,1,128]{2,1,0:T(1,128)S(1)} async-done(((f32[16,1,128]{2,1,0:T(1,128)}), f32[16,1,128]{2,1,0:T(1,128)S(1)}, u32[]{:S(2)}, u32[]{:S(2)}) %all-to-all-start.1) | async-done | bytes 8224 | tf_op jit(solution)/shard_map/all_to_all | solution.py:308
  40.2 1.0 %shard_map.110 = (f32[8,768]{1,0:T(8,128)S(1)}, bf16[16,7,8,128]{3,2,1,0:T(8,128)(2,1)S(1)}) custom-call(f32[16,1,128]{2,1,0:T(1,128)S(1)} %all-to-all-done.1.moments, f32[16,8,128]{2,1,0:T(8,128)S(1)} %get-tuple-element.12.weights, f32[6,8,128]{2,1,0:T(8,128)S(1)} %get-tuple-element.13.rest, f32[8,128]{1,0:T(8,128)S(1)} %get-tuple-element.14.live, ...), custom_call_target="tpu_custom_call" | custom-call | tf_op jit(solution)/shard_map/pallas_call | solution.py:338
  41.2 10.5 %all_to_all.21.received.own = bf16[16,7,8,128]{3,2,1,0:T(8,128)(2,1)S(1)} all-to-all(bf16[16,7,8,128]{3,2,1,0:T(8,128)(2,1)S(1)} %get-tuple-element.15), channel_id=1, replica_groups=mesh['bubble'=16,'panel'=16] {'panel'}, dimensions={0} | all-to-all | bytes 458752 | tf_op jit(solution)/shard_map/all_to_all | solution.py:297
  51.7 0.6 collective-permute-start.2
  52.3 5.4 %collective-permute-done.2.fetched = bf16[16,7,8,128]{3,2,1,0:T(8,128)(2,1)S(1)} collective-permute-done((bf16[16,7,8,128]{3,2,1,0:T(8,128)(2,1)S(1)}, bf16[16,7,8,128]{3,2,1,0:T(8,128)(2,1)S(1)}, u32[]{:S(2)}, u32[]{:S(2)}) %collective-permute-start.2) | collective-permute-done | bytes 229408 | tf_op jit(solution)/shard_map/ppermute | solution.py:298
  57.7 0.0 collective-permute-start.3
  57.7 0.6 moments.3
  58.4 4.6 %all-to-all-start.3 = ((f32[16,1,128]{2,1,0:T(1,128)}), f32[16,1,128]{2,1,0:T(1,128)S(1)}, u32[]{:S(2)}, u32[]{:S(2)}) async-start(f32[16,1,128]{2,1,0:T(1,128)} %moments.3), calls=%async_computation.3 | async-start | bytes 16384 | tf_op jit(solution)/shard_map/all_to_all | solution.py:308
  63.0 0.0 collective-permute-done.3.traded
  63.0 3.1 %shard_map.111 = (f32[6,8,128]{2,1,0:T(8,128)S(1)}, f32[8,128]{1,0:T(8,128)S(1)}) custom-call(s32[6,4,8]{2,1,0:T(4,128)S(1)} %bitcast.10, s32[6,4,8]{2,1,0:T(4,128)S(1)} %bitcast.12, s32[8,6]{1,0:T(8,128)S(1)} %copy-done.7, s32[8]{0:T(128)S(1)} %copy-done.9, f32[3,128]{1,0:T(4,128)S(1)} %copy-done.8, ...), custom_call_target="tpu_custom_call" | custom-call | tf_op jit(solution)/shard_map/pallas_call | solution.py:309
  66.1 6.8 %all-to-all-done.3.moments = f32[16,1,128]{2,1,0:T(1,128)S(1)} async-done(((f32[16,1,128]{2,1,0:T(1,128)}), f32[16,1,128]{2,1,0:T(1,128)S(1)}, u32[]{:S(2)}, u32[]{:S(2)}) %all-to-all-start.3) | async-done | bytes 8224 | tf_op jit(solution)/shard_map/all_to_all | solution.py:308
  72.9 1.4 %shard_map.112 = f32[8,768]{1,0:T(8,128)} custom-call(f32[16,1,128]{2,1,0:T(1,128)S(1)} %all-to-all-done.3.moments, f32[16,8,128]{2,1,0:T(8,128)S(1)} %get-tuple-element.12.weights, f32[6,8,128]{2,1,0:T(8,128)S(1)} %get-tuple-element.16.rest, f32[8,128]{1,0:T(8,128)S(1)} %get-tuple-element.17.live, bf16[128,768]{1,0:T(8,128)(2,1)S(1)} %bitcast.8, ...), custom_call_target="tpu_custom_call" | custom-call | tf_op jit(solution)/shard_map/pallas_call | solution.py:338
  (17 shorter events, 0.0 us)
Async XLA Ops:
  0.0 30.3 %copy-start.3 = (f32[8,768]{1,0:T(8,128)S(1)}, f32[8,768]{1,0:T(8,128)}, u32[]{:S(2)}) copy-start(f32[8,768]{1,0:T(8,128)} %right_side.3) | copy-start | bytes 73732
  0.0 30.3 %copy-start.4 = (s32[8,6,4]{0,2,1:T(4,128)S(1)}, s32[8,6,4]{0,2,1:T(4,128)}, u32[]{:S(2)}) copy-start(s32[8,6,4]{0,2,1:T(4,128)} %param.15) | copy-start | bytes 2308
  0.0 30.3 %copy-start.5 = (s32[8,6,4]{0,2,1:T(4,128)S(1)}, s32[8,6,4]{0,2,1:T(4,128)}, u32[]{:S(2)}) copy-start(s32[8,6,4]{0,2,1:T(4,128)} %param.16) | copy-start | bytes 2308
  0.0 30.3 %copy-start.7 = (s32[8,6]{1,0:T(8,128)S(1)}, s32[8,6]{1,0:T(8,128)}, u32[]{:S(2)}) copy-start(s32[8,6]{1,0:T(8,128)} %near_count_in.3) | copy-start | bytes 580
  0.0 30.3 %copy-start.8 = (f32[3,128]{1,0:T(4,128)S(1)}, f32[3,128]{1,0:T(4,128)}, u32[]{:S(2)}) copy-start(f32[3,128]{1,0:T(4,128)} %centres.3) | copy-start | bytes 4612
  0.0 30.3 %copy-start.9 = (s32[8]{0:T(128)S(1)}, s32[8]{0:T(128)}, u32[]{:S(2)}) copy-start(s32[8]{0:T(128)} %colour_in.3) | copy-start | bytes 100
  1.2 38.9 %copy-start = (bf16[8,6,128,128]{3,2,1,0:T(8,128)(2,1)S(1)}, bf16[8,6,128,128]{3,2,1,0:T(8,128)(2,1)}, u32[]{:S(2)}) copy-start(bf16[8,6,128,128]{3,2,1,0:T(8,128)(2,1)} %inv_diag.3) | copy-start | bytes 4718596
  1.3 38.9 %copy-start.1 = (bf16[8,16,768]{2,1,0:T(8,128)(2,1)S(1)}, bf16[8,16,768]{2,1,0:T(8,128)(2,1)}, u32[]{:S(2)}) copy-start(bf16[8,16,768]{2,1,0:T(8,128)(2,1)} %param.19) | copy-start | bytes 589828
  1.3 38.9 %copy-start.2 = (bf16[8,16,768]{2,1,0:T(8,128)(2,1)S(1)}, bf16[8,16,768]{2,1,0:T(8,128)(2,1)}, u32[]{:S(2)}) copy-start(bf16[8,16,768]{2,1,0:T(8,128)(2,1)} %param.20) | copy-start | bytes 589828
  1.3 38.9 %copy-start.6 = (f32[8,768]{1,0:T(8,128)S(1)}, f32[8,768]{1,0:T(8,128)}, u32[]{:S(2)}) copy-start(f32[8,768]{1,0:T(8,128)} %relaxed.1) | copy-start | bytes 73732
  13.1 6.0 %collective-permute-start = (bf16[16,7,8,128]{3,2,1,0:T(8,128)(2,1)S(1)}, bf16[16,7,8,128]{3,2,1,0:T(8,128)(2,1)S(1)}, u32[]{:S(2)}, u32[]{:S(2)}) collective-permute-start(bf16[16,7,8,128]{3,2,1,0:T(8,128)(2,1)S(1)} %all_to_all.20.received.own), channel_id=1, source_target_pairs={{0,16},{1,3},{2,18},{3,1},{4,20},{5,7},{6,22},{7,5},{8,24},{9,11},... | collective-permute-start | bytes 688136 | tf_op jit(solution)/shard_map/ppermute | solution.py:298
  19.2 11.1 %collective-permute-start.1 = (bf16[16,7,8,128]{3,2,1,0:T(8,128)(2,1)S(1)}, bf16[16,7,8,128]{3,2,1,0:T(8,128)(2,1)S(1)}, u32[]{:S(2)}, u32[]{:S(2)}) collective-permute-start(bf16[16,7,8,128]{3,2,1,0:T(8,128)(2,1)S(1)} %collective-permute-done.fetched), channel_id=1, source_target_pairs={{0,1},{1,0},{2,3},{3,2},{4,5},{5,4},{6,7},{7,6},{8,9},{9,8},{10,11... | collective-permute-start | bytes 688136 | tf_op jit(solution)/shard_map/ppermute | solution.py:299
  19.8 20.4 %all-to-all-start.1 = ((f32[16,1,128]{2,1,0:T(1,128)}), f32[16,1,128]{2,1,0:T(1,128)S(1)}, u32[]{:S(2)}, u32[]{:S(2)}) async-start(f32[16,1,128]{2,1,0:T(1,128)} %moments.2), calls=%async_computation.1 | async-start | bytes 16384 | tf_op jit(solution)/shard_map/all_to_all | solution.py:308
  51.7 6.0 %collective-permute-start.2 = (bf16[16,7,8,128]{3,2,1,0:T(8,128)(2,1)S(1)}, bf16[16,7,8,128]{3,2,1,0:T(8,128)(2,1)S(1)}, u32[]{:S(2)}, u32[]{:S(2)}) collective-permute-start(bf16[16,7,8,128]{3,2,1,0:T(8,128)(2,1)S(1)} %all_to_all.21.received.own), channel_id=1, source_target_pairs={{0,16},{1,3},{2,18},{3,1},{4,20},{5,7},{6,22},{7,5},{8,24},{9,11},... | collective-permute-start | bytes 688136 | tf_op jit(solution)/shard_map/ppermute | solution.py:298
  57.7 5.3 %collective-permute-start.3 = (bf16[16,7,8,128]{3,2,1,0:T(8,128)(2,1)S(1)}, bf16[16,7,8,128]{3,2,1,0:T(8,128)(2,1)S(1)}, u32[]{:S(2)}, u32[]{:S(2)}) collective-permute-start(bf16[16,7,8,128]{3,2,1,0:T(8,128)(2,1)S(1)} %collective-permute-done.2.fetched), channel_id=1, source_target_pairs={{0,1},{1,0},{2,3},{3,2},{4,5},{5,4},{6,7},{7,6},{8,9},{9,8},{10,11... | collective-permute-start | bytes 688136 | tf_op jit(solution)/shard_map/ppermute | solution.py:299
  58.4 14.5 %all-to-all-start.3 = ((f32[16,1,128]{2,1,0:T(1,128)}), f32[16,1,128]{2,1,0:T(1,128)S(1)}, u32[]{:S(2)}, u32[]{:S(2)}) async-start(f32[16,1,128]{2,1,0:T(1,128)} %moments.3), calls=%async_computation.3 | async-start | bytes 16384 | tf_op jit(solution)/shard_map/all_to_all | solution.py:308

commit v3 on v2

--- a/solution.py
+++ b/solution.py
@@ -209,11 +209,11 @@
         cols = slice(r * blk, (r + 1) * blk)
         remainder = rest[r] - far[:, cols]
         updated = jnp.zeros((bub, blk), jnp.float32)
-        for b in range(0, bub, 2):
+        for b in range(0, bub, 4):
             pair = jnp.concatenate(
-                [jnp.where(rows == b + h, remainder, 0.0) for h in range(2)], axis=1
+                [jnp.where(rows == b + h, remainder, 0.0) for h in range(4)], axis=1
             ).astype(jnp.bfloat16)
-            block = jnp.concatenate([inv_diag[b, r], inv_diag[b + 1, r]], axis=1)
+            block = jnp.concatenate([inv_diag[b + h, r] for h in range(4)], axis=1)
             updated = updated + lax.dot_general(
                 pair, block, NT, preferred_element_type=jnp.float32
             )

time: 74.9 us -> 74.9 us (level)
  no operation moved by 1% of the time
where the time goes in v3:
time: 74.9 us; the launch traced here: 74.3 us
  waiting for transfers between devices  23.1 us (31%)
  blocking collectives  22.3 us (30%)
  starting transfers between devices  17.6 us (23%)
  Pallas kernels  11 us (15%)
    all_to_all x2, blocking collectives, per_device(): received = lax.all_to_all(message, 'panel', 0, 0, tiled=True)  22.3 us
    all_to_all x2, starting transfers between devices, per_device(): moments = lax.all_to_all(own_moments, 'bubble', 0, 0, tiled=True)  15.1 us
    all_to_all x2, waiting for transfers between devices, per_device(): moments = lax.all_to_all(own_moments, 'bubble', 0, 0, tiled=True)  13.6 us
    ppermute x2, waiting for transfers between devices, per_device(): fetched = lax.ppermute(received, ('bubble', 'panel'), fetch)  9.52 us
    pallas_call x2, Pallas kernels, per_device(): pl.pallas_call(functools.partial(near_kernel, colour_now), out_shape=near...  6.16 us
    ppermute x2, starting transfers between devices, per_device(): fetched = lax.ppermute(received, ('bubble', 'panel'), fetch)  2.52 us
    pallas_call x2, Pallas kernels, per_device(): pl.pallas_call(functools.partial(finish_kernel, last), out_shape=[relaxed...  2.42 us
  transfers between devices with their start and end apart: 6, of which 4 were waited for; matrix products, arithmetic and copies ran while one was open for 0% of the time, Pallas kernels for 10%

profile of v3, /device:TPU:8, one launch (start us, length us, event | category | flops | bytes accessed | tf_op | source)
XLA Modules:
  0.0 74.3 jit_solution(16868644418899304561)
XLA Ops:
  0.0 1.2 %first.1 = bf16[16,7,8,128]{3,2,1,0:T(8,128)(2,1)S(1)} custom-call(f32[8,768]{1,0:T(8,128)} %relaxed.1, bf16[128,768]{1,0:T(8,128)(2,1)} %bitcast.4), custom_call_target="tpu_custom_call" | custom-call | flops 17179869184 | bytes 1048576 | tf_op jit(solution)/shard_map/first/pallas_call | solution.py:277
  1.2 0.0 copy-start
  1.3 0.0 copy-start.1
  1.3 0.0 copy-start.2
  1.3 0.0 copy-start.6
  1.3 11.8 %all_to_all.20.received.own = bf16[16,7,8,128]{3,2,1,0:T(8,128)(2,1)S(1)} all-to-all(bf16[16,7,8,128]{3,2,1,0:T(8,128)(2,1)S(1)} %first.1), channel_id=1, replica_groups=mesh['bubble'=16,'panel'=16] {'panel'}, dimensions={0} | all-to-all | bytes 458752 | tf_op jit(solution)/shard_map/all_to_all | solution.py:297
  13.1 1.9 %collective-permute-start = (bf16[16,7,8,128]{3,2,1,0:T(8,128)(2,1)S(1)}, bf16[16,7,8,128]{3,2,1,0:T(8,128)(2,1)S(1)}, u32[]{:S(2)}, u32[]{:S(2)}) collective-permute-start(bf16[16,7,8,128]{3,2,1,0:T(8,128)(2,1)S(1)} %all_to_all.20.received.own), channel_id=1, source_target_pairs={{0,16},{1,3},{2,18},{3,1},{4,20},{5,7},{6,22},{7,5},{8,24},{9,11},... | collective-permute-start | bytes 688136 | tf_op jit(solution)/shard_map/ppermute | solution.py:298
  15.1 4.1 %collective-permute-done.fetched = bf16[16,7,8,128]{3,2,1,0:T(8,128)(2,1)S(1)} collective-permute-done((bf16[16,7,8,128]{3,2,1,0:T(8,128)(2,1)S(1)}, bf16[16,7,8,128]{3,2,1,0:T(8,128)(2,1)S(1)}, u32[]{:S(2)}, u32[]{:S(2)}) %collective-permute-start) | collective-permute-done | bytes 229408 | tf_op jit(solution)/shard_map/ppermute | solution.py:298
  19.2 0.0 collective-permute-start.1
  19.2 0.6 moments.2
  19.8 10.5 %all-to-all-start.1 = ((f32[16,1,128]{2,1,0:T(1,128)}), f32[16,1,128]{2,1,0:T(1,128)S(1)}, u32[]{:S(2)}, u32[]{:S(2)}) async-start(f32[16,1,128]{2,1,0:T(1,128)} %moments.2), calls=%async_computation.1 | async-start | bytes 16384 | tf_op jit(solution)/shard_map/all_to_all | solution.py:308
  30.3 3.1 %shard_map.109 = (f32[6,8,128]{2,1,0:T(8,128)S(1)}, f32[8,128]{1,0:T(8,128)S(1)}, f32[16,8,128]{2,1,0:T(8,128)S(1)}) custom-call(s32[6,4,8]{2,1,0:T(4,128)S(1)} %bitcast.9, s32[6,4,8]{2,1,0:T(4,128)S(1)} %bitcast.11, s32[8,6]{1,0:T(8,128)S(1)} %copy-done.7, s32[8]{0:T(128)S(1)} %copy-done.9, f32[3,128]{1,0:T(4,128)S(1)} %copy-done.8, ...), custom_call_target="tpu_custom_call" | custom-call | tf_op jit(solution)/shard_map/pallas_call | solution.py:309
  33.4 6.8 %all-to-all-done.1.moments = f32[16,1,128]{2,1,0:T(1,128)S(1)} async-done(((f32[16,1,128]{2,1,0:T(1,128)}), f32[16,1,128]{2,1,0:T(1,128)S(1)}, u32[]{:S(2)}, u32[]{:S(2)}) %all-to-all-start.1) | async-done | bytes 8224 | tf_op jit(solution)/shard_map/all_to_all | solution.py:308
  40.2 1.0 %shard_map.110 = (f32[8,768]{1,0:T(8,128)S(1)}, bf16[16,7,8,128]{3,2,1,0:T(8,128)(2,1)S(1)}) custom-call(f32[16,1,128]{2,1,0:T(1,128)S(1)} %all-to-all-done.1.moments, f32[16,8,128]{2,1,0:T(8,128)S(1)} %get-tuple-element.12.weights, f32[6,8,128]{2,1,0:T(8,128)S(1)} %get-tuple-element.13.rest, f32[8,128]{1,0:T(8,128)S(1)} %get-tuple-element.14.live, ...), custom_call_target="tpu_custom_call" | custom-call | tf_op jit(solution)/shard_map/pallas_call | solution.py:338
  41.2 10.5 %all_to_all.21.received.own = bf16[16,7,8,128]{3,2,1,0:T(8,128)(2,1)S(1)} all-to-all(bf16[16,7,8,128]{3,2,1,0:T(8,128)(2,1)S(1)} %get-tuple-element.15), channel_id=1, replica_groups=mesh['bubble'=16,'panel'=16] {'panel'}, dimensions={0} | all-to-all | bytes 458752 | tf_op jit(solution)/shard_map/all_to_all | solution.py:297
  51.7 0.6 collective-permute-start.2
  52.3 5.4 %collective-permute-done.2.fetched = bf16[16,7,8,128]{3,2,1,0:T(8,128)(2,1)S(1)} collective-permute-done((bf16[16,7,8,128]{3,2,1,0:T(8,128)(2,1)S(1)}, bf16[16,7,8,128]{3,2,1,0:T(8,128)(2,1)S(1)}, u32[]{:S(2)}, u32[]{:S(2)}) %collective-permute-start.2) | collective-permute-done | bytes 229408 | tf_op jit(solution)/shard_map/ppermute | solution.py:298
  57.7 0.0 collective-permute-start.3
  57.7 0.6 moments.3
  58.4 4.6 %all-to-all-start.3 = ((f32[16,1,128]{2,1,0:T(1,128)}), f32[16,1,128]{2,1,0:T(1,128)S(1)}, u32[]{:S(2)}, u32[]{:S(2)}) async-start(f32[16,1,128]{2,1,0:T(1,128)} %moments.3), calls=%async_computation.3 | async-start | bytes 16384 | tf_op jit(solution)/shard_map/all_to_all | solution.py:308
  63.0 0.0 collective-permute-done.3.traded
  63.0 3.1 %shard_map.111 = (f32[6,8,128]{2,1,0:T(8,128)S(1)}, f32[8,128]{1,0:T(8,128)S(1)}) custom-call(s32[6,4,8]{2,1,0:T(4,128)S(1)} %bitcast.10, s32[6,4,8]{2,1,0:T(4,128)S(1)} %bitcast.12, s32[8,6]{1,0:T(8,128)S(1)} %copy-done.7, s32[8]{0:T(128)S(1)} %copy-done.9, f32[3,128]{1,0:T(4,128)S(1)} %copy-done.8, ...), custom_call_target="tpu_custom_call" | custom-call | tf_op jit(solution)/shard_map/pallas_call | solution.py:309
  66.1 6.8 %all-to-all-done.3.moments = f32[16,1,128]{2,1,0:T(1,128)S(1)} async-done(((f32[16,1,128]{2,1,0:T(1,128)}), f32[16,1,128]{2,1,0:T(1,128)S(1)}, u32[]{:S(2)}, u32[]{:S(2)}) %all-to-all-start.3) | async-done | bytes 8224 | tf_op jit(solution)/shard_map/all_to_all | solution.py:308
  72.9 1.4 %shard_map.112 = f32[8,768]{1,0:T(8,128)} custom-call(f32[16,1,128]{2,1,0:T(1,128)S(1)} %all-to-all-done.3.moments, f32[16,8,128]{2,1,0:T(8,128)S(1)} %get-tuple-element.12.weights, f32[6,8,128]{2,1,0:T(8,128)S(1)} %get-tuple-element.16.rest, f32[8,128]{1,0:T(8,128)S(1)} %get-tuple-element.17.live, bf16[128,768]{1,0:T(8,128)(2,1)S(1)} %bitcast.8, ...), custom_call_target="tpu_custom_call" | custom-call | tf_op jit(solution)/shard_map/pallas_call | solution.py:338
  (17 shorter events, 0.0 us)
Async XLA Ops:
  0.0 30.3 %copy-start.3 = (f32[8,768]{1,0:T(8,128)S(1)}, f32[8,768]{1,0:T(8,128)}, u32[]{:S(2)}) copy-start(f32[8,768]{1,0:T(8,128)} %right_side.3) | copy-start | bytes 73732
  0.0 30.3 %copy-start.4 = (s32[8,6,4]{0,2,1:T(4,128)S(1)}, s32[8,6,4]{0,2,1:T(4,128)}, u32[]{:S(2)}) copy-start(s32[8,6,4]{0,2,1:T(4,128)} %param.15) | copy-start | bytes 2308
  0.0 30.3 %copy-start.5 = (s32[8,6,4]{0,2,1:T(4,128)S(1)}, s32[8,6,4]{0,2,1:T(4,128)}, u32[]{:S(2)}) copy-start(s32[8,6,4]{0,2,1:T(4,128)} %param.16) | copy-start | bytes 2308
  0.0 30.3 %copy-start.7 = (s32[8,6]{1,0:T(8,128)S(1)}, s32[8,6]{1,0:T(8,128)}, u32[]{:S(2)}) copy-start(s32[8,6]{1,0:T(8,128)} %near_count_in.3) | copy-start | bytes 580
  0.0 30.3 %copy-start.8 = (f32[3,128]{1,0:T(4,128)S(1)}, f32[3,128]{1,0:T(4,128)}, u32[]{:S(2)}) copy-start(f32[3,128]{1,0:T(4,128)} %centres.3) | copy-start | bytes 4612
  0.0 30.3 %copy-start.9 = (s32[8]{0:T(128)S(1)}, s32[8]{0:T(128)}, u32[]{:S(2)}) copy-start(s32[8]{0:T(128)} %colour_in.3) | copy-start | bytes 100
  1.2 38.9 %copy-start = (bf16[8,6,128,128]{3,2,1,0:T(8,128)(2,1)S(1)}, bf16[8,6,128,128]{3,2,1,0:T(8,128)(2,1)}, u32[]{:S(2)}) copy-start(bf16[8,6,128,128]{3,2,1,0:T(8,128)(2,1)} %inv_diag.3) | copy-start | bytes 4718596
  1.3 38.9 %copy-start.1 = (bf16[8,16,768]{2,1,0:T(8,128)(2,1)S(1)}, bf16[8,16,768]{2,1,0:T(8,128)(2,1)}, u32[]{:S(2)}) copy-start(bf16[8,16,768]{2,1,0:T(8,128)(2,1)} %param.19) | copy-start | bytes 589828
  1.3 38.9 %copy-start.2 = (bf16[8,16,768]{2,1,0:T(8,128)(2,1)S(1)}, bf16[8,16,768]{2,1,0:T(8,128)(2,1)}, u32[]{:S(2)}) copy-start(bf16[8,16,768]{2,1,0:T(8,128)(2,1)} %param.20) | copy-start | bytes 589828
  1.3 38.9 %copy-start.6 = (f32[8,768]{1,0:T(8,128)S(1)}, f32[8,768]{1,0:T(8,128)}, u32[]{:S(2)}) copy-start(f32[8,768]{1,0:T(8,128)} %relaxed.1) | copy-start | bytes 73732
  13.1 6.0 %collective-permute-start = (bf16[16,7,8,128]{3,2,1,0:T(8,128)(2,1)S(1)}, bf16[16,7,8,128]{3,2,1,0:T(8,128)(2,1)S(1)}, u32[]{:S(2)}, u32[]{:S(2)}) collective-permute-start(bf16[16,7,8,128]{3,2,1,0:T(8,128)(2,1)S(1)} %all_to_all.20.received.own), channel_id=1, source_target_pairs={{0,16},{1,3},{2,18},{3,1},{4,20},{5,7},{6,22},{7,5},{8,24},{9,11},... | collective-permute-start | bytes 688136 | tf_op jit(solution)/shard_map/ppermute | solution.py:298
  19.2 11.1 %collective-permute-start.1 = (bf16[16,7,8,128]{3,2,1,0:T(8,128)(2,1)S(1)}, bf16[16,7,8,128]{3,2,1,0:T(8,128)(2,1)S(1)}, u32[]{:S(2)}, u32[]{:S(2)}) collective-permute-start(bf16[16,7,8,128]{3,2,1,0:T(8,128)(2,1)S(1)} %collective-permute-done.fetched), channel_id=1, source_target_pairs={{0,1},{1,0},{2,3},{3,2},{4,5},{5,4},{6,7},{7,6},{8,9},{9,8},{10,11... | collective-permute-start | bytes 688136 | tf_op jit(solution)/shard_map/ppermute | solution.py:299
  19.8 20.4 %all-to-all-start.1 = ((f32[16,1,128]{2,1,0:T(1,128)}), f32[16,1,128]{2,1,0:T(1,128)S(1)}, u32[]{:S(2)}, u32[]{:S(2)}) async-start(f32[16,1,128]{2,1,0:T(1,128)} %moments.2), calls=%async_computation.1 | async-start | bytes 16384 | tf_op jit(solution)/shard_map/all_to_all | solution.py:308
  51.7 6.0 %collective-permute-start.2 = (bf16[16,7,8,128]{3,2,1,0:T(8,128)(2,1)S(1)}, bf16[16,7,8,128]{3,2,1,0:T(8,128)(2,1)S(1)}, u32[]{:S(2)}, u32[]{:S(2)}) collective-permute-start(bf16[16,7,8,128]{3,2,1,0:T(8,128)(2,1)S(1)} %all_to_all.21.received.own), channel_id=1, source_target_pairs={{0,16},{1,3},{2,18},{3,1},{4,20},{5,7},{6,22},{7,5},{8,24},{9,11},... | collective-permute-start | bytes 688136 | tf_op jit(solution)/shard_map/ppermute | solution.py:298
  57.7 5.3 %collective-permute-start.3 = (bf16[16,7,8,128]{3,2,1,0:T(8,128)(2,1)S(1)}, bf16[16,7,8,128]{3,2,1,0:T(8,128)(2,1)S(1)}, u32[]{:S(2)}, u32[]{:S(2)}) collective-permute-start(bf16[16,7,8,128]{3,2,1,0:T(8,128)(2,1)S(1)} %collective-permute-done.2.fetched), channel_id=1, source_target_pairs={{0,1},{1,0},{2,3},{3,2},{4,5},{5,4},{6,7},{7,6},{8,9},{9,8},{10,11... | collective-permute-start | bytes 688136 | tf_op jit(solution)/shard_map/ppermute | solution.py:299
  58.4 14.5 %all-to-all-start.3 = ((f32[16,1,128]{2,1,0:T(1,128)}), f32[16,1,128]{2,1,0:T(1,128)S(1)}, u32[]{:S(2)}, u32[]{:S(2)}) async-start(f32[16,1,128]{2,1,0:T(1,128)} %moments.3), calls=%async_computation.3 | async-start | bytes 16384 | tf_op jit(solution)/shard_map/all_to_all | solution.py:308
